TPU v7x, 512 devices: a whole 4x8x8 slice. The times are simulated.
512 devices in a mesh: nest: 8 (over x, z_hi), gx: 8 (over y), gy: 8 (over z_lo, core).
Axes of the slice: x: 4, y: 8, z: 8 (z_hi: 2, z_lo: 4; z = z_hi * 4 + z_lo), core: 2. Of those that a mesh axis runs over, the one named last changes fastest.
Arguments:
- state: float32 [8, 4, 8, 128, 1024], P('nest', None, None, 'gx', 'gy'), may hold values from -6 to 6
- metric: float32 [8, 3, 128, 1024], P('nest', None, 'gx', 'gy'), may hold values from -1.2 to 1.4, as said below
- placement: int32 [7, 2], replicated, may hold values from 0 to 682, as said below
- zones: int32 [7, 4], replicated, may hold values from 2 to 5
Outputs:
- new_state: float32 [8, 4, 8, 128, 1024], P('nest', None, None, 'gx', 'gy')
Inputs may be any that keep to these rules, and one draw needn't show every extreme that they name: metric[:, 0] and metric[:, 1] are terrain slopes; metric[:, 2] is the column stretch, between 0.6 and 1.4. placement[n] = (ox, oy) with ox <= 85 and oy <= 682.
All inputs are finite; a program needn't handle non-finite values.
Results may differ from a plain program's by a relative error of at most 0.0003.
Values sent between devices are 32-bit elements; how exact they have to be, the bound alone decides.
No kernel may reach another device: no remote copies, remote signals or barrier semaphores. Data moves between devices by JAX's collectives and lax.ppermute only.
A program may use at most 64 MiB of HBM per device.

v0:
```python
import jax
import jax.numpy as jnp
from jax import lax
from jax.sharding import PartitionSpec as P

SUB = 4
R = 3
W_MAX = 5
WP = 3
TIME_STEP = 0.5
SOUND_SQ = 1.0
PRECISE = lax.Precision.HIGHEST


def extended(value, sides, width):
    for axis, dim in sides:
        devices, length = (lax.axis_size(axis), value.shape[dim])
        up = [(i, (i + 1) % devices) for i in range(devices - 1)]
        down = [(j, i) for i, j in up]
        last = lax.slice_in_dim(value, length - width, length, axis=dim)
        initial = lax.slice_in_dim(value, 0, width, axis=dim)
        before = lax.ppermute(last, axis, up)
        after = lax.ppermute(initial, axis, down)
        value = jnp.concatenate([before, value, after], axis=dim)
    return value


def broadcast(block, axis, owner):
    block = jnp.where(lax.axis_index(axis) == owner, block, jnp.zeros_like(block))
    return lax.psum(block, axis)


def vertical(field):
    upper = jnp.concatenate([field[1:], field[-1:]], 0)
    lower = jnp.concatenate([field[:1], field[:-1]], 0)
    return (upper - lower) * 0.5


def edge_weight(zone_width, row_index, col_index, total_x, total_y):
    widths = zone_width.astype(jnp.float32)
    row_pos = row_index.astype(jnp.float32)[:, None]
    col_pos = col_index.astype(jnp.float32)[None, :]
    dists = (row_pos, total_x - 1 - row_pos, col_pos, total_y - 1 - col_pos)
    weight = jnp.zeros((row_index.shape[0], col_index.shape[0]), jnp.float32)
    for edge in range(4):
        weight = jnp.maximum(weight, jnp.maximum((widths[edge] - dists[edge]) / widths[edge], 0.0))
    return weight


def step_each(current, terrain, sigma_col):
    wind_x, wind_y, updraft, pressure = current
    pressure_ext = extended(pressure, (("gx", 1), ("gy", 2)), 1)
    press_z = vertical(pressure) / terrain[2]
    grad_x = (pressure_ext[:, 2:, 1:-1] - pressure_ext[:, :-2, 1:-1]) * 0.5
    grad_y = (pressure_ext[:, 1:-1, 2:] - pressure_ext[:, 1:-1, :-2]) * 0.5
    new_x = wind_x - TIME_STEP * (grad_x - sigma_col * terrain[0] * press_z)
    new_y = wind_y - TIME_STEP * (grad_y - sigma_col * terrain[1] * press_z)
    new_w = updraft - TIME_STEP * press_z
    winds_ext = extended(jnp.stack([new_x, new_y]), (("gx", 2), ("gy", 3)), 1)
    spread = (winds_ext[0, :, 2:, 1:-1] - winds_ext[0, :, :-2, 1:-1]) * 0.5 + (
        winds_ext[1, :, 1:-1, 2:] - winds_ext[1, :, 1:-1, :-2]
    ) * 0.5
    spread = (
        spread
        - sigma_col * (terrain[0] * vertical(new_x) + terrain[1] * vertical(new_y)) / terrain[2]
        + vertical(new_w) / terrain[2]
    )
    return (new_x, new_y, new_w, pressure - TIME_STEP * SOUND_SQ * spread)


def boundary_pieces(
    parent_tile, placement, row_start, col_start, total_x, total_y, foot_x, foot_y, span_len
):
    row_index = row_start + jnp.arange(parent_tile.shape[2], dtype=jnp.int32)
    col_index = col_start + jnp.arange(parent_tile.shape[3], dtype=jnp.int32)
    depth_range = jnp.arange(WP, dtype=jnp.int32)
    reach_range = jnp.arange(span_len, dtype=jnp.int32)
    west_x = placement[:, 0:1]
    south_y = placement[:, 1:2]
    east_base = (total_x - 1) // R - (WP - 1)
    north_base = (total_y - 1) // R - (WP - 1)
    x_depth = jnp.stack([west_x + depth_range, west_x + east_base + depth_range], 1)
    y_depth = jnp.stack([south_y + depth_range, south_y + north_base + depth_range], 1)
    x_reach = jnp.where(reach_range < foot_x, west_x + reach_range, -1)
    y_reach = jnp.where(reach_range < foot_y, south_y + reach_range, -1)
    pick_rows = (x_depth[..., None] == row_index).astype(jnp.float32)
    pick_cols = (y_reach[:, None, :] == col_index[None, :, None]).astype(jnp.float32)
    across = jnp.einsum("neai,flij->neflaj", pick_rows, parent_tile, precision=PRECISE)
    across = jnp.einsum("neflaj,njb->neflab", across, pick_cols, precision=PRECISE)
    pick_depth = (y_depth[..., None] == col_index).astype(jnp.float32)
    pick_reach = (x_reach[:, None, :] == row_index[None, :, None]).astype(jnp.float32)
    along_y = jnp.einsum("neaj,flij->neflai", pick_depth, parent_tile, precision=PRECISE)
    along_y = jnp.einsum("neflai,nib->neflab", along_y, pick_reach, precision=PRECISE)
    return jnp.concatenate([across, along_y], 1)


def relax_edges(relaxed_in, own_pieces, zone_width, row_start, col_start, total_x, total_y, active):
    row_index = row_start + jnp.arange(relaxed_in.shape[2], dtype=jnp.int32)
    col_index = col_start + jnp.arange(relaxed_in.shape[3], dtype=jnp.int32)
    depth_range = jnp.arange(WP, dtype=jnp.int32)
    reach_range = jnp.arange(own_pieces.shape[-1], dtype=jnp.int32)
    east_base = (total_x - 1) // R - (WP - 1)
    north_base = (total_y - 1) // R - (WP - 1)
    west_pick = ((row_index < W_MAX)[:, None] & ((row_index // R)[:, None] == depth_range)).astype(
        jnp.float32
    )
    east_pick = (
        (row_index >= total_x - W_MAX)[:, None]
        & ((row_index // R - east_base)[:, None] == depth_range)
    ).astype(jnp.float32)
    south_pick = ((col_index < W_MAX)[:, None] & ((col_index // R)[:, None] == depth_range)).astype(
        jnp.float32
    )
    north_pick = (
        (col_index >= total_y - W_MAX)[:, None]
        & ((col_index // R - north_base)[:, None] == depth_range)
    ).astype(jnp.float32)
    col_reach = (reach_range[:, None] == (col_index // R)[None, :]).astype(jnp.float32)
    row_reach = (reach_range[:, None] == (row_index // R)[None, :]).astype(jnp.float32)
    across = jnp.einsum("eflab,bj->eflaj", own_pieces[0:2], col_reach, precision=PRECISE)
    from_x = jnp.einsum("ia,flaj->flij", west_pick, across[0], precision=PRECISE) + jnp.einsum(
        "ia,flaj->flij", east_pick, across[1], precision=PRECISE
    )
    along_y = jnp.einsum("eflab,bi->eflai", own_pieces[2:4], row_reach, precision=PRECISE)
    from_y = jnp.einsum("ja,flai->flij", south_pick, along_y[0], precision=PRECISE) + jnp.einsum(
        "ja,flai->flij", north_pick, along_y[1], precision=PRECISE
    )
    in_x = (row_index < W_MAX) | (row_index >= total_x - W_MAX)
    target = jnp.where(in_x[:, None], from_x, from_y)
    weight = edge_weight(zone_width, row_index, col_index, total_x, total_y)
    weight = jnp.where(active, weight, 0.0)
    return relaxed_in + weight * (target - relaxed_in)


def local(state, metric, placement, zones):
    fields = state[0]
    terrain = metric[0]
    levels, size_x, size_y = (fields.shape[1], fields.shape[2], fields.shape[3])
    total_x = size_x * lax.axis_size("gx")
    total_y = size_y * lax.axis_size("gy")
    nest_count = placement.shape[0]
    group_index = lax.axis_index("nest")
    row_start = lax.axis_index("gx") * size_x
    col_start = lax.axis_index("gy") * size_y
    foot_x = (total_x + R - 1) // R
    foot_y = (total_y + R - 1) // R
    span_len = 64 * ((max(foot_x, foot_y) + 63) // 64)
    own_group = jnp.minimum(group_index, nest_count - 1)
    start_three = jnp.stack([fields[0], fields[1], fields[3]])
    pieces = boundary_pieces(
        start_three, placement, row_start, col_start, total_x, total_y, foot_x, foot_y, span_len
    )
    summed = lax.psum(pieces, ("gx", "gy"))
    arrived = broadcast(summed, "nest", nest_count)
    own_pieces = arrived[own_group]
    sigma_col = (1.0 - (jnp.arange(levels, dtype=jnp.float32) + 0.5) / levels)[:, None, None]
    current = (fields[0], fields[1], fields[2], fields[3])
    for substep in range(SUB):
        current = step_each(current, terrain, sigma_col)
    active = group_index < nest_count
    moved_three = jnp.stack([current[0], current[1], current[3]])
    relaxed = relax_edges(
        moved_three, own_pieces, zones[own_group], row_start, col_start, total_x, total_y, active
    )
    result = jnp.stack([relaxed[0], relaxed[1], current[2], relaxed[2]])
    return result[None]


def solution(mesh):
    return jax.shard_map(
        local,
        mesh=mesh,
        in_specs=(P("nest", None, None, "gx", "gy"), P("nest", None, "gx", "gy"), P(), P()),
        out_specs=P("nest", None, None, "gx", "gy"),
        check_vma=False,
    )
```

profile of v0, /device:TPU:1, one launch (start us, length us, event | category | flops | bytes accessed | tf_op | source)
XLA Modules:
  0.0 865.6 jit_solution(14164995903394578647)
XLA Ops:
  11.9 1.9 pad_maximum_fusion
  13.9 4.2 collective-permute-start.1
  18.1 1.3 collective-permute-start
  20.3 1.4 divide_maximum_fusion
  23.2 5.4 collective-permute-start.3
  28.5 2.5 collective-permute-start.2
  31.2 3.3 collective-permute-done.2
  34.7 1.3 collective-permute-start.4
  36.0 4.4 collective-permute-start.5
  41.3 2.7 collective-permute-start.7
  44.0 1.9 collective-permute-start.6
  46.7 5.1 collective-permute-done.6
  52.0 3.6 collective-permute-start.9
  55.7 1.3 collective-permute-start.8
  57.0 5.0 collective-permute-done.8
  62.1 2.5 collective-permute-start.11
  64.6 1.9 collective-permute-start.10
  66.7 3.9 collective-permute-done.10
  70.8 1.3 collective-permute-start.12
  72.1 5.1 collective-permute-start.13
  78.1 2.7 collective-permute-start.15
  80.8 1.9 collective-permute-start.14
  83.4 4.7 collective-permute-done.14
  88.3 6.4 collective-permute-start.17
  94.7 1.3 collective-permute-start.16
  96.0 3.9 collective-permute-done.16
  100.1 2.1 collective-permute-start.19
  102.2 2.2 collective-permute-start.18
  104.5 4.1 collective-permute-done.18
  108.8 1.3 collective-permute-start.20
  110.1 4.9 collective-permute-start.21
  115.9 2.7 collective-permute-start.23
  118.6 1.9 collective-permute-start.22
  121.5 6.1 collective-permute-done.22
  127.8 4.3 collective-permute-start.25
  132.1 1.3 collective-permute-start.24
  133.5 438.1 %all-reduce.3.cloned.1.call-done = f32[7,4,3,8,3,384]{5,3,4,2,1,0:T(8,128)} async-done(((f32[7,4,3,8,3,384]{5,3,4,2,1,0:T(8,128)}), f32[7,4,3,8,3,384]{5,3,4,2,1,0:T(8,128)}) %all-reduce.3.cloned.1.call-update) | async-done | bytes 3096592 | tf_op jit(solution)/shard_map/psum | solution.py:153
  571.6 1.9 broadcast_select_fusion
  573.7 1.9 collective-permute-start.27
  575.6 3.8 collective-permute-start.26
  579.4 2.1 collective-permute-done.26
  581.7 1.3 collective-permute-start.28
  583.0 4.0 collective-permute-start.29
  588.0 3.0 collective-permute-start.31
  590.9 1.9 collective-permute-start.30
  592.9 5.6 collective-permute-done.31
  598.5 62.3 %collective-permute-done.30 = f32[2,8,18,1]{3,2,1,0:T(8,128)S(1)} collective-permute-done((f32[2,8,18,1]{3,2,1,0:T(8,128)S(1)}, f32[2,8,18,1]{3,2,1,0:T(8,128)S(1)}, u32[]{:S(2)}, u32[]{:S(2)}) %collective-permute-start.30) | collective-permute-done | bytes 1184 | tf_op jit(solution)/shard_map/ppermute | solution.py:23
  661.1 193.1 %all-reduce.5.cloned.1.call-done = f32[7,4,3,8,3,384]{5,3,4,2,1,0:T(8,128)} async-done(((f32[7,4,3,8,3,384]{5,3,4,2,1,0:T(8,128)}), f32[7,4,3,8,3,384]{5,3,4,2,1,0:T(8,128)}) %all-reduce.5.cloned.1.call-update) | async-done | bytes 3096592 | tf_op jit(solution)/shard_map/psum | solution.py:30
  (143 shorter events, 20.5 us)
Async XLA Ops:
  6.5 565.0 %all-reduce.3.cloned.1.call-start = ((), (), s32[]{:S(2)}) async-start(), calls=%async_computation | async-start | bytes 6193152 | tf_op jit(solution)/shard_map/psum | solution.py:153
  13.8 5.7 copy-start
  13.8 5.7 copy-start.1
  13.8 5.8 copy-start.2
  13.8 840.3 %all-reduce.5.cloned.1.call-start = ((), (), s32[]{:S(2)}) async-start(), calls=%async_computation.1 | async-start | bytes 6193152 | tf_op jit(solution)/shard_map/psum | solution.py:30
  13.9 9.1 %collective-permute-start.1 = (f32[8,1,128]{2,1,0:T(1,128)S(1)}, f32[8,1,128]{2,1,0:T(1,128)S(1)}, u32[]{:S(2)}, u32[]{:S(2)}) collective-permute-start(f32[8,1,128]{2,1,0:T(1,128)S(1)} %get-tuple-element.182), channel_id=1, source_target_pairs={{0,8},{8,16},{16,24},{24,32},{32,40},{40,48},{48,56},{1,9},{9,17},... | collective-permute-start | bytes 12296 | tf_op jit(solution)/shard_map/ppermute | solution.py:22
  18.1 5.0 collective-permute-start
  23.2 8.0 collective-permute-start.3
  28.5 5.9 collective-permute-start.2
  34.7 5.7 collective-permute-start.4
  36.0 5.2 collective-permute-start.5
  41.3 5.5 collective-permute-start.7
  44.0 7.8 collective-permute-start.6
  52.0 5.0 collective-permute-start.9
  55.7 6.3 collective-permute-start.8
  62.1 4.6 collective-permute-start.11
  64.6 5.9 collective-permute-start.10
  70.8 6.4 collective-permute-start.12
  72.1 5.8 collective-permute-start.13
  78.1 5.3 collective-permute-start.15
  80.8 7.3 collective-permute-start.14
  88.3 7.7 collective-permute-start.17
  94.7 5.2 collective-permute-start.16
  100.1 4.5 collective-permute-start.19
  102.2 6.4 collective-permute-start.18
  108.8 6.3 collective-permute-start.20
  110.1 5.7 collective-permute-start.21
  115.9 5.5 collective-permute-start.23
  118.6 9.0 %collective-permute-start.22 = (f32[2,8,18,1]{3,2,1,0:T(8,128)S(1)}, f32[2,8,18,1]{3,2,1,0:T(8,128)S(1)}, u32[]{:S(2)}, u32[]{:S(2)}) collective-permute-start(f32[2,8,18,1]{3,2,1,0:T(8,128)S(1)} %get-tuple-element.35), channel_id=1, source_target_pairs={{1,0},{2,1},{3,2},{4,3},{5,4},{6,5},{7,6},{9,8},{10,9},{11,10},{12... | collective-permute-start | bytes 3464 | tf_op jit(solution)/shard_map/ppermute | solution.py:23
  127.8 445.8 %collective-permute-start.25 = (f32[8,1,128]{2,1,0:T(1,128)S(1)}, f32[8,1,128]{2,1,0:T(1,128)S(1)}, u32[]{:S(2)}, u32[]{:S(2)}) collective-permute-start(f32[8,1,128]{2,1,0:T(1,128)S(1)} %get-tuple-element.171), channel_id=1, source_target_pairs={{0,8},{8,16},{16,24},{24,32},{32,40},{40,48},{48,56},{1,9},{9,17},... | collective-permute-start | bytes 12296 | tf_op jit(solution)/shard_map/ppermute | solution.py:22
  132.1 441.5 %collective-permute-start.24 = (f32[8,1,128]{2,1,0:T(1,128)S(1)}, f32[8,1,128]{2,1,0:T(1,128)S(1)}, u32[]{:S(2)}, u32[]{:S(2)}) collective-permute-start(f32[8,1,128]{2,1,0:T(1,128)S(1)} %get-tuple-element.172), channel_id=1, source_target_pairs={{8,0},{16,8},{24,16},{32,24},{40,32},{48,40},{56,48},{9,1},{17,9},... | collective-permute-start | bytes 12296 | tf_op jit(solution)/shard_map/ppermute | solution.py:23
  573.7 5.7 collective-permute-start.27
  575.6 5.9 collective-permute-start.26
  581.7 5.3 collective-permute-start.28
  583.0 4.8 collective-permute-start.29
  588.0 10.5 %collective-permute-start.31 = (f32[2,8,18,1]{3,2,1,0:T(8,128)S(1)}, f32[2,8,18,1]{3,2,1,0:T(8,128)S(1)}, u32[]{:S(2)}, u32[]{:S(2)}) collective-permute-start(f32[2,8,18,1]{3,2,1,0:T(8,128)S(1)} %get-tuple-element.34), channel_id=1, source_target_pairs={{0,1},{1,2},{2,3},{3,4},{4,5},{5,6},{6,7},{8,9},{9,10},{10,11},{11... | collective-permute-start | bytes 3464 | tf_op jit(solution)/shard_map/ppermute | solution.py:22
  590.9 69.9 %collective-permute-start.30 = (f32[2,8,18,1]{3,2,1,0:T(8,128)S(1)}, f32[2,8,18,1]{3,2,1,0:T(8,128)S(1)}, u32[]{:S(2)}, u32[]{:S(2)}) collective-permute-start(f32[2,8,18,1]{3,2,1,0:T(8,128)S(1)} %get-tuple-element.33), channel_id=1, source_target_pairs={{1,0},{2,1},{3,2},{4,3},{5,4},{6,5},{7,6},{9,8},{10,9},{11,10},{12... | collective-permute-start | bytes 3464 | tf_op jit(solution)/shard_map/ppermute | solution.py:23
Sparse Core Ops, SparseCore 0:
  14.0 557.5 all-reduce.2
  574.5 279.5 all-reduce.4
where the time goes:
time: 867 us; the launch traced here: 866 us
  waiting for transfers between devices  743 us (86%)
  starting transfers between devices  88.2 us (10%)
  between operations  14.5 us (2%)
  other arithmetic  10.4 us (1%)
    psum x1, waiting for transfers between devices, local(): summed = lax.psum(pieces, ('gx', 'gy'))  438 us
    psum x1, waiting for transfers between devices, broadcast(): return lax.psum(block, axis)  193 us
    ppermute x16, waiting for transfers between devices, extended(): after = lax.ppermute(initial, axis, down)  100 us
    ppermute x16, starting transfers between devices, extended(): before = lax.ppermute(last, axis, up)  59.8 us
    ppermute x16, starting transfers between devices, extended(): after = lax.ppermute(initial, axis, down)  28.4 us
  transfers between devices with their start and end apart: 34, of which 20 were waited for; matrix products, arithmetic and copies ran while one was open for 1% of the time, Pallas kernels for 0%

commit v1 on v0

--- a/solution.py
+++ b/solution.py
@@ -150,7 +150,7 @@
     pieces = boundary_pieces(
         start_three, placement, row_start, col_start, total_x, total_y, foot_x, foot_y, span_len
     )
-    summed = lax.psum(pieces, ("gx", "gy"))
+    summed = lax.psum(lax.psum(pieces, "gx"), "gy")
     arrived = broadcast(summed, "nest", nest_count)
     own_pieces = arrived[own_group]
     sigma_col = (1.0 - (jnp.arange(levels, dtype=jnp.float32) + 0.5) / levels)[:, None, None]

time: 867 us -> 507 us (0.58)
  waiting for transfers between devices: 743 us -> 381 us
    psum x1 -> x2, waiting for transfers between devices: 438 us -> 83.6 us  [local(): summed = lax.psum(lax.psum(pieces, 'gx'), 'gy')]
    ppermute x16, waiting for transfers between devices: 100 us -> 40.4 us  [extended(): after = lax.ppermute(initial, axis, down)]
    psum x1, waiting for transfers between devices: 193 us -> 245 us  [broadcast(): return lax.psum(block, axis)]
  transfers between devices with their start and end apart: 34 -> 35, of which waited for: 20 -> 20; matrix products, arithmetic and copies ran while one was open for 1% -> 2% of each run, Pallas kernels for 0% -> 0%
where the time goes in v1:
time: 507 us; the launch traced here: 506 us
  waiting for transfers between devices  381 us (75%)
  starting transfers between devices  90.7 us (18%)
  between operations  14.2 us (3%)
  other arithmetic  10.4 us (2%)
  matrix products  6.91 us (1%)
    psum x1, waiting for transfers between devices, broadcast(): return lax.psum(block, axis)  245 us
    psum x2, waiting for transfers between devices, local(): summed = lax.psum(lax.psum(pieces, 'gx'), 'gy')  83.6 us
    ppermute x16, starting transfers between devices, extended(): before = lax.ppermute(last, axis, up)  62.6 us
    ppermute x16, waiting for transfers between devices, extended(): after = lax.ppermute(initial, axis, down)  40.4 us
    ppermute x16, starting transfers between devices, extended(): after = lax.ppermute(initial, axis, down)  28.1 us
    ppermute x16, waiting for transfers between devices, extended(): before = lax.ppermute(last, axis, up)  12.2 us
  transfers between devices with their start and end apart: 35, of which 20 were waited for; matrix products, arithmetic and copies ran while one was open for 2% of the time, Pallas kernels for 0%

profile of v1, /device:TPU:1, one launch (start us, length us, event | category | flops | bytes accessed | tf_op | source)
XLA Modules:
  0.0 506.2 jit_solution(11141159930112730367)
XLA Ops:
  11.9 1.9 pad_maximum_fusion
  13.9 4.2 collective-permute-start.1
  18.1 1.3 collective-permute-start
  20.3 1.4 divide_maximum_fusion
  23.2 5.4 %collective-permute-start.3 = (f32[8,18,1]{2,1,0:T(8,128)S(1)}, f32[8,18,1]{2,1,0:T(8,128)S(1)}, u32[]{:S(2)}, u32[]{:S(2)}) collective-permute-start(f32[8,18,1]{2,1,0:T(8,128)S(1)} %get-tuple-element.58), channel_id=1, source_target_pairs={{0,1},{1,2},{2,3},{3,4},{4,5},{5,6},{6,7},{8,9},{9,10},{10,11},{11... | collective-permute-start | bytes 1736 | tf_op jit(solution)/shard_map/ppermute | solution.py:22
  28.5 2.5 collective-permute-start.2
  31.2 3.3 collective-permute-done.2
  34.7 1.3 collective-permute-start.4
  36.0 4.4 collective-permute-start.5
  41.3 2.7 collective-permute-start.7
  44.0 1.9 collective-permute-start.6
  46.5 5.2 %collective-permute-done.6 = f32[2,8,18,1]{3,2,1,0:T(8,128)S(1)} collective-permute-done((f32[2,8,18,1]{3,2,1,0:T(8,128)S(1)}, f32[2,8,18,1]{3,2,1,0:T(8,128)S(1)}, u32[]{:S(2)}, u32[]{:S(2)}) %collective-permute-start.6) | collective-permute-done | bytes 1184 | tf_op jit(solution)/shard_map/ppermute | solution.py:23
  51.9 4.1 collective-permute-start.9
  56.0 1.3 collective-permute-start.8
  57.3 4.4 collective-permute-done.8
  61.8 2.0 collective-permute-start.11
  63.8 2.3 collective-permute-start.10
  66.3 4.1 collective-permute-done.10
  70.5 1.3 collective-permute-start.12
  71.8 5.2 %collective-permute-start.13 = (f32[2,8,1,128]{3,2,1,0:T(1,128)S(1)}, f32[2,8,1,128]{3,2,1,0:T(1,128)S(1)}, u32[]{:S(2)}, u32[]{:S(2)}) collective-permute-start(f32[2,8,1,128]{3,2,1,0:T(1,128)S(1)} %get-tuple-element.47), channel_id=1, source_target_pairs={{0,8},{8,16},{16,24},{24,32},{32,40},{40,48},{48,56},{1,9},{9,17},... | collective-permute-start | bytes 24584 | tf_op jit(solution)/shard_map/ppermute | solution.py:22
  77.9 2.7 collective-permute-start.15
  80.6 1.9 collective-permute-start.14
  83.2 4.8 collective-permute-done.14
  88.2 5.4 %collective-permute-start.17 = (f32[8,1,128]{2,1,0:T(1,128)S(1)}, f32[8,1,128]{2,1,0:T(1,128)S(1)}, u32[]{:S(2)}, u32[]{:S(2)}) collective-permute-start(f32[8,1,128]{2,1,0:T(1,128)S(1)} %get-tuple-element.176), channel_id=1, source_target_pairs={{0,8},{8,16},{16,24},{24,32},{32,40},{40,48},{48,56},{1,9},{9,17},... | collective-permute-start | bytes 12296 | tf_op jit(solution)/shard_map/ppermute | solution.py:22
  93.6 1.3 collective-permute-start.16
  94.9 4.6 collective-permute-done.16
  99.7 2.2 collective-permute-start.19
  101.8 2.2 collective-permute-start.18
  104.0 11.3 %all-reduce.4.cloned.1.call-done = f32[7,4,3,8,3,384]{5,3,4,2,1,0:T(8,128)} async-done(((f32[7,4,3,8,3,384]{5,3,4,2,1,0:T(8,128)}), f32[7,4,3,8,3,384]{5,3,4,2,1,0:T(8,128)}) %all-reduce.4.cloned.1.call-update) | async-done | bytes 3096592 | tf_op jit(solution)/shard_map/psum | solution.py:153
  115.7 1.3 collective-permute-start.20
  117.0 4.0 collective-permute-start.21
  121.9 6.2 %collective-permute-start.23 = (f32[2,8,18,1]{3,2,1,0:T(8,128)S(1)}, f32[2,8,18,1]{3,2,1,0:T(8,128)S(1)}, u32[]{:S(2)}, u32[]{:S(2)}) collective-permute-start(f32[2,8,18,1]{3,2,1,0:T(8,128)S(1)} %get-tuple-element.36), channel_id=1, source_target_pairs={{0,1},{1,2},{2,3},{3,4},{4,5},{5,6},{6,7},{8,9},{9,10},{10,11},{11... | collective-permute-start | bytes 3464 | tf_op jit(solution)/shard_map/ppermute | solution.py:22
  128.1 1.9 collective-permute-start.22
  130.7 4.8 collective-permute-done.22
  135.7 5.5 %collective-permute-start.25 = (f32[8,1,128]{2,1,0:T(1,128)S(1)}, f32[8,1,128]{2,1,0:T(1,128)S(1)}, u32[]{:S(2)}, u32[]{:S(2)}) collective-permute-start(f32[8,1,128]{2,1,0:T(1,128)S(1)} %get-tuple-element.171), channel_id=1, source_target_pairs={{0,8},{8,16},{16,24},{24,32},{32,40},{40,48},{48,56},{1,9},{9,17},... | collective-permute-start | bytes 12296 | tf_op jit(solution)/shard_map/ppermute | solution.py:22
  141.3 1.3 collective-permute-start.24
  142.6 72.3 %all-reduce.6.cloned.1.call-done = f32[7,4,3,8,3,384]{5,3,4,2,1,0:T(8,128)} async-done(((f32[7,4,3,8,3,384]{5,3,4,2,1,0:T(8,128)}), f32[7,4,3,8,3,384]{5,3,4,2,1,0:T(8,128)}) %all-reduce.6.cloned.1.call-update) | async-done | bytes 3096592 | tf_op jit(solution)/shard_map/psum | solution.py:153
  214.9 1.8 broadcast_select_fusion
  217.0 1.9 collective-permute-start.27
  219.0 3.1 collective-permute-start.26
  222.1 2.8 collective-permute-done.26
  225.1 1.3 collective-permute-start.28
  226.4 4.0 collective-permute-start.29
  231.3 3.0 collective-permute-start.31
  234.3 1.9 collective-permute-start.30
  236.2 7.4 %collective-permute-done.31 = f32[2,8,18,1]{3,2,1,0:T(8,128)S(1)} collective-permute-done((f32[2,8,18,1]{3,2,1,0:T(8,128)S(1)}, f32[2,8,18,1]{3,2,1,0:T(8,128)S(1)}, u32[]{:S(2)}, u32[]{:S(2)}) %collective-permute-start.31) | collective-permute-done | bytes 1184 | tf_op jit(solution)/shard_map/ppermute | solution.py:22
  243.6 6.4 %collective-permute-done.30 = f32[2,8,18,1]{3,2,1,0:T(8,128)S(1)} collective-permute-done((f32[2,8,18,1]{3,2,1,0:T(8,128)S(1)}, f32[2,8,18,1]{3,2,1,0:T(8,128)S(1)}, u32[]{:S(2)}, u32[]{:S(2)}) %collective-permute-start.30) | collective-permute-done | bytes 1184 | tf_op jit(solution)/shard_map/ppermute | solution.py:23
  250.3 244.8 %all-reduce.8.cloned.1.call-done = f32[7,4,3,8,3,384]{5,3,4,2,1,0:T(8,128)} async-done(((f32[7,4,3,8,3,384]{5,3,4,2,1,0:T(8,128)}), f32[7,4,3,8,3,384]{5,3,4,2,1,0:T(8,128)}) %all-reduce.8.cloned.1.call-update) | async-done | bytes 3096592 | tf_op jit(solution)/shard_map/psum | solution.py:30
  (146 shorter events, 20.1 us)
Async XLA Ops:
  6.5 108.8 %all-reduce.4.cloned.1.call-start = ((), (), s32[]{:S(2)}) async-start(), calls=%async_computation | async-start | bytes 6193152 | tf_op jit(solution)/shard_map/psum | solution.py:153
  13.8 5.7 %copy-start = (f32[1,4,8,16,128]{4,3,2,1,0:T(8,128)S(1)}, f32[1,4,8,16,128]{4,3,2,1,0:T(8,128)}, u32[]{:S(2)}) copy-start(f32[1,4,8,16,128]{4,3,2,1,0:T(8,128)} %param.4) | copy-start | bytes 786436
  13.8 5.7 %copy-start.1 = (f32[1,3,16,128]{3,2,1,0:T(8,128)S(1)}, f32[1,3,16,128]{3,2,1,0:T(8,128)}, u32[]{:S(2)}) copy-start(f32[1,3,16,128]{3,2,1,0:T(8,128)} %param.5) | copy-start | bytes 73732
  13.8 5.8 %copy-start.2 = (s32[7,4]{0,1:T(4,128)S(1)}, s32[7,4]{0,1:T(4,128)}, u32[]{:S(2)}) copy-start(s32[7,4]{0,1:T(4,128)} %param.7) | copy-start | bytes 340
  13.8 201.1 %all-reduce.6.cloned.1.call-start = ((), (), s32[]{:S(2)}) async-start(), calls=%async_computation.1 | async-start | bytes 6193152 | tf_op jit(solution)/shard_map/psum | solution.py:153
  13.9 9.1 %collective-permute-start.1 = (f32[8,1,128]{2,1,0:T(1,128)S(1)}, f32[8,1,128]{2,1,0:T(1,128)S(1)}, u32[]{:S(2)}, u32[]{:S(2)}) collective-permute-start(f32[8,1,128]{2,1,0:T(1,128)S(1)} %get-tuple-element.182), channel_id=1, source_target_pairs={{0,8},{8,16},{16,24},{24,32},{32,40},{40,48},{48,56},{1,9},{9,17},... | collective-permute-start | bytes 12296 | tf_op jit(solution)/shard_map/ppermute | solution.py:22
  18.1 5.0 collective-permute-start
  23.2 8.0 %collective-permute-start.3 = (f32[8,18,1]{2,1,0:T(8,128)S(1)}, f32[8,18,1]{2,1,0:T(8,128)S(1)}, u32[]{:S(2)}, u32[]{:S(2)}) collective-permute-start(f32[8,18,1]{2,1,0:T(8,128)S(1)} %get-tuple-element.58), channel_id=1, source_target_pairs={{0,1},{1,2},{2,3},{3,4},{4,5},{5,6},{6,7},{8,9},{9,10},{10,11},{11... | collective-permute-start | bytes 1736 | tf_op jit(solution)/shard_map/ppermute | solution.py:22
  28.5 5.9 %collective-permute-start.2 = (f32[8,18,1]{2,1,0:T(8,128)S(1)}, f32[8,18,1]{2,1,0:T(8,128)S(1)}, u32[]{:S(2)}, u32[]{:S(2)}) collective-permute-start(f32[8,18,1]{2,1,0:T(8,128)S(1)} %get-tuple-element.57), channel_id=1, source_target_pairs={{1,0},{2,1},{3,2},{4,3},{5,4},{6,5},{7,6},{9,8},{10,9},{11,10},{12... | collective-permute-start | bytes 1736 | tf_op jit(solution)/shard_map/ppermute | solution.py:23
  34.7 5.7 %collective-permute-start.4 = (f32[2,8,1,128]{3,2,1,0:T(1,128)S(1)}, f32[2,8,1,128]{3,2,1,0:T(1,128)S(1)}, u32[]{:S(2)}, u32[]{:S(2)}) collective-permute-start(f32[2,8,1,128]{3,2,1,0:T(1,128)S(1)} %get-tuple-element.50), channel_id=1, source_target_pairs={{8,0},{16,8},{24,16},{32,24},{40,32},{48,40},{56,48},{9,1},{17,9},... | collective-permute-start | bytes 24584 | tf_op jit(solution)/shard_map/ppermute | solution.py:23
  36.0 5.2 %collective-permute-start.5 = (f32[2,8,1,128]{3,2,1,0:T(1,128)S(1)}, f32[2,8,1,128]{3,2,1,0:T(1,128)S(1)}, u32[]{:S(2)}, u32[]{:S(2)}) collective-permute-start(f32[2,8,1,128]{3,2,1,0:T(1,128)S(1)} %get-tuple-element.49), channel_id=1, source_target_pairs={{0,8},{8,16},{16,24},{24,32},{32,40},{40,48},{48,56},{1,9},{9,17},... | collective-permute-start | bytes 24584 | tf_op jit(solution)/shard_map/ppermute | solution.py:22
  41.3 5.3 %collective-permute-start.7 = (f32[2,8,18,1]{3,2,1,0:T(8,128)S(1)}, f32[2,8,18,1]{3,2,1,0:T(8,128)S(1)}, u32[]{:S(2)}, u32[]{:S(2)}) collective-permute-start(f32[2,8,18,1]{3,2,1,0:T(8,128)S(1)} %get-tuple-element.40), channel_id=1, source_target_pairs={{0,1},{1,2},{2,3},{3,4},{4,5},{5,6},{6,7},{8,9},{9,10},{10,11},{11... | collective-permute-start | bytes 3464 | tf_op jit(solution)/shard_map/ppermute | solution.py:22
  44.0 7.8 %collective-permute-start.6 = (f32[2,8,18,1]{3,2,1,0:T(8,128)S(1)}, f32[2,8,18,1]{3,2,1,0:T(8,128)S(1)}, u32[]{:S(2)}, u32[]{:S(2)}) collective-permute-start(f32[2,8,18,1]{3,2,1,0:T(8,128)S(1)} %get-tuple-element.39), channel_id=1, source_target_pairs={{1,0},{2,1},{3,2},{4,3},{5,4},{6,5},{7,6},{9,8},{10,9},{11,10},{12... | collective-permute-start | bytes 3464 | tf_op jit(solution)/shard_map/ppermute | solution.py:23
  51.9 5.4 %collective-permute-start.9 = (f32[8,1,128]{2,1,0:T(1,128)S(1)}, f32[8,1,128]{2,1,0:T(1,128)S(1)}, u32[]{:S(2)}, u32[]{:S(2)}) collective-permute-start(f32[8,1,128]{2,1,0:T(1,128)S(1)} %get-tuple-element.180), channel_id=1, source_target_pairs={{0,8},{8,16},{16,24},{24,32},{32,40},{40,48},{48,56},{1,9},{9,17},... | collective-permute-start | bytes 12296 | tf_op jit(solution)/shard_map/ppermute | solution.py:22
  56.0 5.7 %collective-permute-start.8 = (f32[8,1,128]{2,1,0:T(1,128)S(1)}, f32[8,1,128]{2,1,0:T(1,128)S(1)}, u32[]{:S(2)}, u32[]{:S(2)}) collective-permute-start(f32[8,1,128]{2,1,0:T(1,128)S(1)} %get-tuple-element.179), channel_id=1, source_target_pairs={{8,0},{16,8},{24,16},{32,24},{40,32},{48,40},{56,48},{9,1},{17,9},... | collective-permute-start | bytes 12296 | tf_op jit(solution)/shard_map/ppermute | solution.py:23
  61.8 4.5 collective-permute-start.11
  63.8 6.5 %collective-permute-start.10 = (f32[8,18,1]{2,1,0:T(8,128)S(1)}, f32[8,18,1]{2,1,0:T(8,128)S(1)}, u32[]{:S(2)}, u32[]{:S(2)}) collective-permute-start(f32[8,18,1]{2,1,0:T(8,128)S(1)} %get-tuple-element.55), channel_id=1, source_target_pairs={{1,0},{2,1},{3,2},{4,3},{5,4},{6,5},{7,6},{9,8},{10,9},{11,10},{12... | collective-permute-start | bytes 1736 | tf_op jit(solution)/shard_map/ppermute | solution.py:23
  70.5 6.6 %collective-permute-start.12 = (f32[2,8,1,128]{3,2,1,0:T(1,128)S(1)}, f32[2,8,1,128]{3,2,1,0:T(1,128)S(1)}, u32[]{:S(2)}, u32[]{:S(2)}) collective-permute-start(f32[2,8,1,128]{3,2,1,0:T(1,128)S(1)} %get-tuple-element.48), channel_id=1, source_target_pairs={{8,0},{16,8},{24,16},{32,24},{40,32},{48,40},{56,48},{9,1},{17,9},... | collective-permute-start | bytes 24584 | tf_op jit(solution)/shard_map/ppermute | solution.py:23
  71.8 6.0 %collective-permute-start.13 = (f32[2,8,1,128]{3,2,1,0:T(1,128)S(1)}, f32[2,8,1,128]{3,2,1,0:T(1,128)S(1)}, u32[]{:S(2)}, u32[]{:S(2)}) collective-permute-start(f32[2,8,1,128]{3,2,1,0:T(1,128)S(1)} %get-tuple-element.47), channel_id=1, source_target_pairs={{0,8},{8,16},{16,24},{24,32},{32,40},{40,48},{48,56},{1,9},{9,17},... | collective-permute-start | bytes 24584 | tf_op jit(solution)/shard_map/ppermute | solution.py:22
  77.9 5.3 %collective-permute-start.15 = (f32[2,8,18,1]{3,2,1,0:T(8,128)S(1)}, f32[2,8,18,1]{3,2,1,0:T(8,128)S(1)}, u32[]{:S(2)}, u32[]{:S(2)}) collective-permute-start(f32[2,8,18,1]{3,2,1,0:T(8,128)S(1)} %get-tuple-element.38), channel_id=1, source_target_pairs={{0,1},{1,2},{2,3},{3,4},{4,5},{5,6},{6,7},{8,9},{9,10},{10,11},{11... | collective-permute-start | bytes 3464 | tf_op jit(solution)/shard_map/ppermute | solution.py:22
  80.6 7.4 %collective-permute-start.14 = (f32[2,8,18,1]{3,2,1,0:T(8,128)S(1)}, f32[2,8,18,1]{3,2,1,0:T(8,128)S(1)}, u32[]{:S(2)}, u32[]{:S(2)}) collective-permute-start(f32[2,8,18,1]{3,2,1,0:T(8,128)S(1)} %get-tuple-element.37), channel_id=1, source_target_pairs={{1,0},{2,1},{3,2},{4,3},{5,4},{6,5},{7,6},{9,8},{10,9},{11,10},{12... | collective-permute-start | bytes 3464 | tf_op jit(solution)/shard_map/ppermute | solution.py:23
  88.2 6.7 %collective-permute-start.17 = (f32[8,1,128]{2,1,0:T(1,128)S(1)}, f32[8,1,128]{2,1,0:T(1,128)S(1)}, u32[]{:S(2)}, u32[]{:S(2)}) collective-permute-start(f32[8,1,128]{2,1,0:T(1,128)S(1)} %get-tuple-element.176), channel_id=1, source_target_pairs={{0,8},{8,16},{16,24},{24,32},{32,40},{40,48},{48,56},{1,9},{9,17},... | collective-permute-start | bytes 12296 | tf_op jit(solution)/shard_map/ppermute | solution.py:22
  93.6 6.0 %collective-permute-start.16 = (f32[8,1,128]{2,1,0:T(1,128)S(1)}, f32[8,1,128]{2,1,0:T(1,128)S(1)}, u32[]{:S(2)}, u32[]{:S(2)}) collective-permute-start(f32[8,1,128]{2,1,0:T(1,128)S(1)} %get-tuple-element.175), channel_id=1, source_target_pairs={{8,0},{16,8},{24,16},{32,24},{40,32},{48,40},{56,48},{9,1},{17,9},... | collective-permute-start | bytes 12296 | tf_op jit(solution)/shard_map/ppermute | solution.py:23
  99.7 15.8 %collective-permute-start.19 = (f32[8,18,1]{2,1,0:T(8,128)S(1)}, f32[8,18,1]{2,1,0:T(8,128)S(1)}, u32[]{:S(2)}, u32[]{:S(2)}) collective-permute-start(f32[8,18,1]{2,1,0:T(8,128)S(1)} %get-tuple-element.54), channel_id=1, source_target_pairs={{0,1},{1,2},{2,3},{3,4},{4,5},{5,6},{6,7},{8,9},{9,10},{10,11},{11... | collective-permute-start | bytes 1736 | tf_op jit(solution)/shard_map/ppermute | solution.py:22
  101.8 13.7 %collective-permute-start.18 = (f32[8,18,1]{2,1,0:T(8,128)S(1)}, f32[8,18,1]{2,1,0:T(8,128)S(1)}, u32[]{:S(2)}, u32[]{:S(2)}) collective-permute-start(f32[8,18,1]{2,1,0:T(8,128)S(1)} %get-tuple-element.53), channel_id=1, source_target_pairs={{1,0},{2,1},{3,2},{4,3},{5,4},{6,5},{7,6},{9,8},{10,9},{11,10},{12... | collective-permute-start | bytes 1736 | tf_op jit(solution)/shard_map/ppermute | solution.py:23
  115.3 379.8 %all-reduce.8.cloned.1.call-start = ((), (), s32[]{:S(2)}) async-start(), calls=%async_computation.2 | async-start | bytes 6193152 | tf_op jit(solution)/shard_map/psum | solution.py:30
  115.7 5.4 %collective-permute-start.20 = (f32[2,8,1,128]{3,2,1,0:T(1,128)S(1)}, f32[2,8,1,128]{3,2,1,0:T(1,128)S(1)}, u32[]{:S(2)}, u32[]{:S(2)}) collective-permute-start(f32[2,8,1,128]{3,2,1,0:T(1,128)S(1)} %get-tuple-element.46), channel_id=1, source_target_pairs={{8,0},{16,8},{24,16},{32,24},{40,32},{48,40},{56,48},{9,1},{17,9},... | collective-permute-start | bytes 24584 | tf_op jit(solution)/shard_map/ppermute | solution.py:23
  117.0 4.8 collective-permute-start.21
  121.9 8.8 %collective-permute-start.23 = (f32[2,8,18,1]{3,2,1,0:T(8,128)S(1)}, f32[2,8,18,1]{3,2,1,0:T(8,128)S(1)}, u32[]{:S(2)}, u32[]{:S(2)}) collective-permute-start(f32[2,8,18,1]{3,2,1,0:T(8,128)S(1)} %get-tuple-element.36), channel_id=1, source_target_pairs={{0,1},{1,2},{2,3},{3,4},{4,5},{5,6},{6,7},{8,9},{9,10},{10,11},{11... | collective-permute-start | bytes 3464 | tf_op jit(solution)/shard_map/ppermute | solution.py:22
  128.1 7.4 %collective-permute-start.22 = (f32[2,8,18,1]{3,2,1,0:T(8,128)S(1)}, f32[2,8,18,1]{3,2,1,0:T(8,128)S(1)}, u32[]{:S(2)}, u32[]{:S(2)}) collective-permute-start(f32[2,8,18,1]{3,2,1,0:T(8,128)S(1)} %get-tuple-element.35), channel_id=1, source_target_pairs={{1,0},{2,1},{3,2},{4,3},{5,4},{6,5},{7,6},{9,8},{10,9},{11,10},{12... | collective-permute-start | bytes 3464 | tf_op jit(solution)/shard_map/ppermute | solution.py:23
  135.7 81.2 %collective-permute-start.25 = (f32[8,1,128]{2,1,0:T(1,128)S(1)}, f32[8,1,128]{2,1,0:T(1,128)S(1)}, u32[]{:S(2)}, u32[]{:S(2)}) collective-permute-start(f32[8,1,128]{2,1,0:T(1,128)S(1)} %get-tuple-element.171), channel_id=1, source_target_pairs={{0,8},{8,16},{16,24},{24,32},{32,40},{40,48},{48,56},{1,9},{9,17},... | collective-permute-start | bytes 12296 | tf_op jit(solution)/shard_map/ppermute | solution.py:22
  141.3 75.6 %collective-permute-start.24 = (f32[8,1,128]{2,1,0:T(1,128)S(1)}, f32[8,1,128]{2,1,0:T(1,128)S(1)}, u32[]{:S(2)}, u32[]{:S(2)}) collective-permute-start(f32[8,1,128]{2,1,0:T(1,128)S(1)} %get-tuple-element.172), channel_id=1, source_target_pairs={{8,0},{16,8},{24,16},{32,24},{40,32},{48,40},{56,48},{9,1},{17,9},... | collective-permute-start | bytes 12296 | tf_op jit(solution)/shard_map/ppermute | solution.py:23
  217.0 5.1 collective-permute-start.27
  219.0 5.9 %collective-permute-start.26 = (f32[8,18,1]{2,1,0:T(8,128)S(1)}, f32[8,18,1]{2,1,0:T(8,128)S(1)}, u32[]{:S(2)}, u32[]{:S(2)}) collective-permute-start(f32[8,18,1]{2,1,0:T(8,128)S(1)} %get-tuple-element.51), channel_id=1, source_target_pairs={{1,0},{2,1},{3,2},{4,3},{5,4},{6,5},{7,6},{9,8},{10,9},{11,10},{12... | collective-permute-start | bytes 1736 | tf_op jit(solution)/shard_map/ppermute | solution.py:23
  225.1 5.3 %collective-permute-start.28 = (f32[2,8,1,128]{3,2,1,0:T(1,128)S(1)}, f32[2,8,1,128]{3,2,1,0:T(1,128)S(1)}, u32[]{:S(2)}, u32[]{:S(2)}) collective-permute-start(f32[2,8,1,128]{3,2,1,0:T(1,128)S(1)} %get-tuple-element.44), channel_id=1, source_target_pairs={{8,0},{16,8},{24,16},{32,24},{40,32},{48,40},{56,48},{9,1},{17,9},... | collective-permute-start | bytes 24584 | tf_op jit(solution)/shard_map/ppermute | solution.py:23
  226.4 4.8 collective-permute-start.29
  231.3 12.3 %collective-permute-start.31 = (f32[2,8,18,1]{3,2,1,0:T(8,128)S(1)}, f32[2,8,18,1]{3,2,1,0:T(8,128)S(1)}, u32[]{:S(2)}, u32[]{:S(2)}) collective-permute-start(f32[2,8,18,1]{3,2,1,0:T(8,128)S(1)} %get-tuple-element.34), channel_id=1, source_target_pairs={{0,1},{1,2},{2,3},{3,4},{4,5},{5,6},{6,7},{8,9},{9,10},{10,11},{11... | collective-permute-start | bytes 3464 | tf_op jit(solution)/shard_map/ppermute | solution.py:22
  234.3 15.7 %collective-permute-start.30 = (f32[2,8,18,1]{3,2,1,0:T(8,128)S(1)}, f32[2,8,18,1]{3,2,1,0:T(8,128)S(1)}, u32[]{:S(2)}, u32[]{:S(2)}) collective-permute-start(f32[2,8,18,1]{3,2,1,0:T(8,128)S(1)} %get-tuple-element.33), channel_id=1, source_target_pairs={{1,0},{2,1},{3,2},{4,3},{5,4},{6,5},{7,6},{9,8},{10,9},{11,10},{12... | collective-permute-start | bytes 3464 | tf_op jit(solution)/shard_map/ppermute | solution.py:23
Sparse Core Ops, SparseCore 0:
  14.0 101.2 all-reduce.3
  118.3 96.6 all-reduce.5
  217.9 277.1 all-reduce.7
